TPU v7x, 32 devices: a whole 2x2x4 slice. The times are simulated.
32 devices in a mesh: grp: 4 (over y, core), row: 8 (over z, x).
Axes of the slice: x: 2, y: 2, z: 4, core: 2. Of those that a mesh axis runs over, the one named last changes fastest.
Arguments:
- landmarks: bfloat16 [1024, 1024], P(('grp', 'row')), may hold values from -6.5 to 6.5
- initial_basis: bfloat16 [1024, 256], P(('grp', 'row')), may hold values from -0.1875 to 0.1875
- points: bfloat16 [32768, 1024], P(('grp', 'row')), may hold values from -6.5 to 6.5
Outputs:
- basis: float32 [1024, 256], P(('grp', 'row'))
- coords: float32 [32768, 256], P(('grp', 'row'))
All inputs are finite; a program needn't handle non-finite values.
Results may differ from a plain program's by a relative error of at most 0.0057.
Values may be sent and summed in bfloat16 or wider, within the bound.
No kernel may reach another device: no remote copies, remote signals or barrier semaphores. Data moves between devices by JAX's collectives and lax.ppermute only.
A program may use at most 128 MiB of HBM per device.

v0:
```python
import math
import jax
import jax.numpy as jnp
from jax import lax
from jax.sharding import PartitionSpec as P

ITERS = 2
spread = 0.25


def squared_rows(rows):
    return jnp.sum(jnp.square(rows.astype(jnp.float32)), axis=1)


def pair_kernel(left, right):
    inner = lax.dot_general(
        left, right, (((1,), (1,)), ((), ())), preferred_element_type=jnp.float32
    )
    dist = squared_rows(left)[:, None] + squared_rows(right)[None, :] - 2.0 * inner
    return jnp.exp(-dist / (spread * left.shape[1]))


def point_terms(anchors, spectral_rows, members, member_sq):
    inner = lax.dot_general(
        anchors, members, (((1,), (1,)), ((), ())), preferred_element_type=jnp.float32
    )
    dist = squared_rows(anchors)[:, None] + member_sq[None, :] - 2.0 * inner
    kernel_part = jnp.exp(-dist / (spread * anchors.shape[1]))
    degree_part = jnp.sum(kernel_part, axis=0)
    numer_part = lax.dot_general(
        kernel_part.astype(jnp.bfloat16),
        spectral_rows,
        (((0,), (0,)), ((), ())),
        preferred_element_type=jnp.float32,
    )
    return (numer_part, degree_part)


def body(landmarks, initial_basis, points):
    local_rows = landmarks.shape[0]
    total = local_rows * lax.axis_size("grp") * lax.axis_size("row")
    row_index = lax.axis_index("row")
    group_rows = lax.all_gather(landmarks, "row", axis=0, tiled=True)
    cross_rows = lax.all_gather(landmarks, "grp", axis=0, tiled=True)
    land_kernel = pair_kernel(group_rows, cross_rows)
    group_degree = lax.psum(jnp.sum(land_kernel, axis=1), "row")
    own_degree = lax.dynamic_slice_in_dim(group_degree, row_index * local_rows, local_rows, 0)
    cross_degree = lax.psum(jnp.sum(land_kernel, axis=0), "grp")
    row_scale = 1.0 / jnp.sqrt(group_degree)
    column_scale = 1.0 / jnp.sqrt(cross_degree)
    affinity = (land_kernel * row_scale[:, None] * column_scale[None, :]).astype(jnp.bfloat16)
    current = initial_basis
    for step in range(ITERS):
        cross_basis = lax.all_gather(current, "grp", axis=0, tiled=True)
        image = lax.psum_scatter(
            jnp.dot(affinity, cross_basis, preferred_element_type=jnp.float32),
            "row",
            scatter_dimension=0,
            tiled=True,
        )
        gram = lax.psum(jnp.dot(image.T, image, precision=lax.Precision.HIGHEST), ("grp", "row"))
        lower = jnp.linalg.cholesky(gram)
        ortho = jax.scipy.linalg.solve_triangular(lower, image.T, lower=True).T
        current = ortho.astype(jnp.bfloat16)
    lam = jnp.diagonal(lower)
    own_scale = 1.0 / jnp.sqrt(own_degree)
    spectral = (ortho * own_scale[:, None] / lam[None, :]).astype(jnp.bfloat16)
    point_sq = squared_rows(points)
    numer_part, degree_part = point_terms(
        lax.all_gather(landmarks, ("grp", "row"), axis=0, tiled=True),
        lax.all_gather(spectral, ("grp", "row"), axis=0, tiled=True),
        points,
        point_sq,
    )
    coords = numer_part / jnp.sqrt(degree_part)[:, None] * math.sqrt(total)
    return (ortho, coords)


def solution(mesh):
    in_specs = (P(("grp", "row"), None), P(("grp", "row"), None), P(("grp", "row"), None))
    out_specs = (P(("grp", "row"), None), P(("grp", "row"), None))
    return jax.shard_map(body, mesh=mesh, in_specs=in_specs, out_specs=out_specs, check_vma=False)
```

profile of v0, /device:TPU:0, one launch (start us, length us, event | category | flops | bytes accessed | tf_op | source)
XLA Modules:
  0.0 683.4 jit_solution(5649184369802876398)
XLA Ops:
  7.2 7.5 %all_gather.19 = bf16[128,1024]{1,0:T(8,128)(2,1)S(1)} all-gather(bf16[32,1024]{1,0:T(8,128)(2,1)} %param.6), channel_id=1, replica_groups=mesh['grp'=4,'row'=8] {'grp'}, dimensions={0}, use_global_device_ids=true | all-gather | bytes 327680 | tf_op jit(solution)/shard_map/all_gather | solution.py:44
  14.7 32.1 %all_gather.18 = bf16[256,1024]{1,0:T(8,128)(2,1)S(1)} all-gather(bf16[32,1024]{1,0:T(8,128)(2,1)} %param.6), channel_id=1, replica_groups=mesh['grp'=4,'row'=8] {'row'}, dimensions={0}, use_global_device_ids=true | all-gather | bytes 589824 | tf_op jit(solution)/shard_map/all_gather | solution.py:43
  46.7 5.4 all_gather.20
  52.9 21.4 %psum.28 = f32[256]{0:T(256)S(1)} all-reduce(f32[256]{0:T(256)S(1)} %get-tuple-element.20), channel_id=1, replica_groups=mesh['grp'=4,'row'=8] {'row'}, use_global_device_ids=true, to_apply=%region_3.0 | all-reduce | flops 256 | bytes 2048 | tf_op jit(solution)/shard_map/psum | solution.py:46
  74.3 5.7 psum.29
  80.9 59.6 %reduce-scatter.3.cloned.1.call-done = f32[32,256]{1,0:T(8,128)} async-done(((f32[256,256]{1,0:T(8,128)}), f32[32,256]{1,0:T(8,128)}) %reduce-scatter.3.cloned.1.call-update) | async-done | bytes 32784 | tf_op jit(solution)/shard_map/reduce_scatter | solution.py:55
  142.6 129.7 %all-reduce.4.cloned.1.call-done = f32[256,256]{0,1:T(8,128)} async-done(((f32[256,256]{0,1:T(8,128)}), f32[256,256]{0,1:T(8,128)}) %all-reduce.4.cloned.1.call-update) | async-done | bytes 262160 | tf_op jit(solution)/shard_map/psum | solution.py:61
  274.4 11.7 %cholesky.130 = f32[128,128]{1,0:T(8,128)S(1)} custom-call(f32[128,128]{1,0:T(8,128)S(1)} %cholesky.194), custom_call_target="Cholesky" | custom-call | tf_op jit(solution)/shard_map/jit(cholesky)/cholesky | solution.py:62
  286.2 9.8 %custom-call.15 = f32[1,128,128]{1,2,0:T(8,128)S(1)} custom-call(f32[1,128,128]{2,1,0:T(8,128)S(1)} %get-tuple-element.53), custom_call_target="InvertDiagBlocksLowerTriangular" | custom-call | tf_op jit(solution)/shard_map/jit(cholesky)/cholesky | solution.py:62
  296.5 11.7 %cholesky.147 = f32[128,128]{1,0:T(8,128)S(1)} custom-call(f32[128,128]{1,0:T(8,128)S(1)} %convolution_subtract_fusion.1), custom_call_target="Cholesky" | custom-call | tf_op jit(solution)/shard_map/jit(cholesky)/cholesky | solution.py:62
  310.4 4.3 while.4
  314.7 19.7 %custom-call.16 = f32[2,128,128]{1,2,0:T(8,128)S(1)} custom-call(f32[2,128,128]{2,1,0:T(8,128)S(1)} %get-tuple-element.18), custom_call_target="InvertDiagBlocksLowerTriangular" | custom-call | tf_op jit(solution)/shard_map/jit(_solve_triangular)/triangular_solve | solution.py:63
  335.0 5.2 all_gather.21
  341.3 61.2 %reduce-scatter.5.cloned.1.call-done = f32[32,256]{1,0:T(8,128)} async-done(((f32[256,256]{1,0:T(8,128)}), f32[32,256]{1,0:T(8,128)}) %reduce-scatter.5.cloned.1.call-update) | async-done | bytes 32784 | tf_op jit(solution)/shard_map/reduce_scatter | solution.py:55
  405.7 128.4 %all-reduce.6.cloned.1.call-done = f32[256,256]{0,1:T(8,128)} async-done(((f32[256,256]{0,1:T(8,128)}), f32[256,256]{0,1:T(8,128)}) %all-reduce.6.cloned.1.call-update) | async-done | bytes 262160 | tf_op jit(solution)/shard_map/psum | solution.py:61
  536.1 11.7 %cholesky.164 = f32[128,128]{1,0:T(8,128)S(1)} custom-call(f32[128,128]{1,0:T(8,128)S(1)} %cholesky.197), custom_call_target="Cholesky" | custom-call | tf_op jit(solution)/shard_map/jit(cholesky)/cholesky | solution.py:62
  547.9 9.8 %custom-call.17 = f32[1,128,128]{1,2,0:T(8,128)S(1)} custom-call(f32[1,128,128]{2,1,0:T(8,128)S(1)} %get-tuple-element.49), custom_call_target="InvertDiagBlocksLowerTriangular" | custom-call | tf_op jit(solution)/shard_map/jit(cholesky)/cholesky | solution.py:62
  558.2 11.7 %cholesky.181 = f32[128,128]{1,0:T(8,128)S(1)} custom-call(f32[128,128]{1,0:T(8,128)S(1)} %convolution_subtract_fusion), custom_call_target="Cholesky" | custom-call | tf_op jit(solution)/shard_map/jit(cholesky)/cholesky | solution.py:62
  572.6 4.2 while.5
  576.8 19.7 %custom-call.18 = f32[2,128,128]{1,2,0:T(8,128)S(1)} custom-call(f32[2,128,128]{2,1,0:T(8,128)S(1)} %get-tuple-element.19), custom_call_target="InvertDiagBlocksLowerTriangular" | custom-call | tf_op jit(solution)/shard_map/jit(_solve_triangular)/triangular_solve | solution.py:63
  596.4 2.3 gather_fusion
  600.0 68.2 %all_gather.23 = bf16[1024,256]{1,0:T(8,128)(2,1)S(1)} all-gather(bf16[32,256]{1,0:T(8,128)(2,1)S(1)} %get-tuple-element.38), channel_id=1, replica_groups=mesh['grp'=4,'row'=8] {'grp','row'}, dimensions={0}, use_global_device_ids=true | all-gather | bytes 540672 | tf_op jit(solution)/shard_map/all_gather | solution.py:71
  670.3 4.3 fusion
  674.6 2.3 divide_multiply_fusion
  (76 shorter events, 27.1 us)
Async XLA Ops:
  7.2 133.4 %reduce-scatter.3.cloned.1.call-start = ((), (), s32[]{:S(2)}) async-start(), calls=%async_computation.2 | async-start | bytes 294912 | tf_op jit(solution)/shard_map/reduce_scatter | solution.py:55
  52.5 352.7 %copy-start = (bf16[1024,1024]{1,0:T(8,128)(2,1)S(1)}, bf16[1024,1024]{1,0:T(8,128)(2,1)}, u32[]{:S(2)}) copy-start(bf16[1024,1024]{1,0:T(8,128)(2,1)} %param.8) | copy-start | bytes 6291460
  80.9 191.5 %all-reduce.4.cloned.1.call-start = ((), (), s32[]{:S(2)}) async-start(), calls=%async_computation.3 | async-start | bytes 524288 | tf_op jit(solution)/shard_map/psum | solution.py:61
  140.6 193.8 %copy-start.2 = (f32[32,256]{1,0:T(8,128)S(1)}, f32[32,256]{1,0:T(8,128)}, u32[]{:S(2)}) copy-start(f32[32,256]{1,0:T(8,128)} %reduce-scatter.3.cloned.1.call-done) | copy-start | bytes 98308
  142.6 259.9 %reduce-scatter.5.cloned.1.call-start = ((), (), s32[]{:S(2)}) async-start(), calls=%async_computation.4 | async-start | bytes 294912 | tf_op jit(solution)/shard_map/reduce_scatter | solution.py:55
  341.2 192.9 %all-reduce.6.cloned.1.call-start = ((), (), s32[]{:S(2)}) async-start(), calls=%async_computation.5 | async-start | bytes 524288 | tf_op jit(solution)/shard_map/psum | solution.py:61
  402.5 196.3 %copy-start.1 = (f32[32,256]{1,0:T(8,128)S(1)}, f32[32,256]{1,0:T(8,128)}, u32[]{:S(2)}) copy-start(f32[32,256]{1,0:T(8,128)} %reduce-scatter.5.cloned.1.call-done) | copy-start | bytes 98308
  404.5 263.7 %all-gather.2.cloned.1.call-start = ((), (), s32[]{:S(2)}) async-start(), calls=%async_computation.6 | async-start | bytes 2162688 | tf_op jit(solution)/shard_map/all_gather | solution.py:70
Sparse Core Ops, SparseCore 0:
  81.0 59.5 reduce-scatter.2
  146.7 125.6 all-reduce.3
  341.3 61.1 reduce-scatter.4
  408.4 125.5 all-reduce.5
  536.9 56.1 all-gather.1
where the time goes:
time: 684 us; the launch traced here: 683 us
  waiting for transfers between devices  380 us (56%)
  blocking collectives  145 us (21%)
  other arithmetic  114 us (17%)
  between operations  16.7 us (2%)
  matrix products  14.9 us (2%)
  local copies, waits for them, and re-layouts  12.7 us (2%)
    psum x2, waiting for transfers between devices, body(): lax.psum(jnp.dot(image.T, image, precision=lax.Precision.HIGHEST), ('grp'...  258 us
    reduce_scatter x2, waiting for transfers between devices, body(): lax.psum_scatter(jnp.dot(affinity, cross_basis, preferred_element_type=jn...  121 us
    another operation x13, other arithmetic, body(): lower = jnp.linalg.cholesky(gram)  68.6 us
    all_gather x1, blocking collectives, body(): lax.all_gather(spectral, ('grp', 'row'), axis=0, tiled=True)  68.2 us
    another operation x5, other arithmetic, body(): ortho = jax.scipy.linalg.solve_triangular(lower, image.T, lower=True).T  39.4 us
    all_gather x1, blocking collectives, body(): group_rows = lax.all_gather(landmarks, 'row', axis=0, tiled=True)  32.1 us
    psum x1, blocking collectives, body(): group_degree = lax.psum(jnp.sum(land_kernel, axis=1), 'row')  21.4 us
  transfers between devices with their start and end apart: 5, of which 4 were waited for; matrix products, arithmetic and copies ran while one was open for 9% of the time, Pallas kernels for 0%

commit v1 on v0

--- a/solution.py
+++ b/solution.py
@@ -6,6 +6,11 @@
 
 ITERS = 2
 spread = 0.25
+
+
+def all_by_exchange(value, mesh_axis, along):
+    sent = jnp.stack([value] * lax.axis_size(mesh_axis))
+    return jnp.concatenate(lax.all_to_all(sent, mesh_axis, 0, 0), axis=along)
 
 
 def squared_rows(rows):
@@ -68,7 +73,7 @@
     point_sq = squared_rows(points)
     numer_part, degree_part = point_terms(
         lax.all_gather(landmarks, ("grp", "row"), axis=0, tiled=True),
-        lax.all_gather(spectral, ("grp", "row"), axis=0, tiled=True),
+        all_by_exchange(spectral, ("grp", "row"), 0),
         points,
         point_sq,
     )

time: 684 us -> 633 us (0.925)
  blocking collectives: 145 us -> 77.1 us
  waiting for transfers between devices: 380 us -> 388 us
    all_gather x1 -> x0, blocking collectives: 68.2 us -> none  [body(): lax.all_gather(spectral, ('grp', 'row'), axis=0, tiled=True)]
    all_to_all x0 -> x1, waiting for transfers between devices: none -> 7.47 us  [all_by_exchange(): return jnp.concatenate(lax.all_to_all(sent, mesh_axis, 0, 0), axis=along)]
  transfers between devices with their start and end apart: 5 -> 6, of which waited for: 4 -> 5; matrix products, arithmetic and copies ran while one was open for 9% -> 12% of each run, Pallas kernels for 0% -> 0%
where the time goes in v1:
time: 633 us; the launch traced here: 632 us
  waiting for transfers between devices  388 us (61%)
  other arithmetic  114 us (18%)
  blocking collectives  77.1 us (12%)
  matrix products  18.8 us (3%)
  between operations  16.8 us (3%)
  local copies, waits for them, and re-layouts  13.7 us (2%)
    psum x2, waiting for transfers between devices, body(): lax.psum(jnp.dot(image.T, image, precision=lax.Precision.HIGHEST), ('grp'...  259 us
    reduce_scatter x2, waiting for transfers between devices, body(): lax.psum_scatter(jnp.dot(affinity, cross_basis, preferred_element_type=jn...  121 us
    another operation x13, other arithmetic, body(): lower = jnp.linalg.cholesky(gram)  68.7 us
    another operation x5, other arithmetic, body(): ortho = jax.scipy.linalg.solve_triangular(lower, image.T, lower=True).T  39.4 us
    all_gather x1, blocking collectives, body(): group_rows = lax.all_gather(landmarks, 'row', axis=0, tiled=True)  32.1 us
    psum x1, blocking collectives, body(): group_degree = lax.psum(jnp.sum(land_kernel, axis=1), 'row')  21.2 us
  transfers between devices with their start and end apart: 6, of which 5 were waited for; matrix products, arithmetic and copies ran while one was open for 12% of the time, Pallas kernels for 0%

profile of v1, /device:TPU:0, one launch (start us, length us, event | category | flops | bytes accessed | tf_op | source)
XLA Modules:
  0.0 631.9 jit_solution(7932173201342315546)
XLA Ops:
  7.2 7.5 %all_gather.16 = bf16[128,1024]{1,0:T(8,128)(2,1)S(1)} all-gather(bf16[32,1024]{1,0:T(8,128)(2,1)} %param.6), channel_id=1, replica_groups=mesh['grp'=4,'row'=8] {'grp'}, dimensions={0}, use_global_device_ids=true | all-gather | bytes 327680 | tf_op jit(solution)/shard_map/all_gather | solution.py:49
  14.7 32.1 %all_gather.15 = bf16[256,1024]{1,0:T(8,128)(2,1)S(1)} all-gather(bf16[32,1024]{1,0:T(8,128)(2,1)} %param.6), channel_id=1, replica_groups=mesh['grp'=4,'row'=8] {'row'}, dimensions={0}, use_global_device_ids=true | all-gather | bytes 589824 | tf_op jit(solution)/shard_map/all_gather | solution.py:48
  46.7 5.4 all_gather.17
  52.9 21.2 %psum.28 = f32[256]{0:T(256)S(1)} all-reduce(f32[256]{0:T(256)S(1)} %get-tuple-element.20), channel_id=1, replica_groups=mesh['grp'=4,'row'=8] {'row'}, use_global_device_ids=true, to_apply=%region_3.0 | all-reduce | flops 256 | bytes 2048 | tf_op jit(solution)/shard_map/psum | solution.py:51
  74.1 5.7 psum.29
  80.8 59.6 %reduce-scatter.3.cloned.1.call-done = f32[32,256]{1,0:T(8,128)} async-done(((f32[256,256]{1,0:T(8,128)}), f32[32,256]{1,0:T(8,128)}) %reduce-scatter.3.cloned.1.call-update) | async-done | bytes 32784 | tf_op jit(solution)/shard_map/reduce_scatter | solution.py:60
  142.5 129.7 %all-reduce.4.cloned.1.call-done = f32[256,256]{0,1:T(8,128)} async-done(((f32[256,256]{0,1:T(8,128)}), f32[256,256]{0,1:T(8,128)}) %all-reduce.4.cloned.1.call-update) | async-done | bytes 262160 | tf_op jit(solution)/shard_map/psum | solution.py:66
  274.3 11.7 %cholesky.130 = f32[128,128]{1,0:T(8,128)S(1)} custom-call(f32[128,128]{1,0:T(8,128)S(1)} %cholesky.194), custom_call_target="Cholesky" | custom-call | tf_op jit(solution)/shard_map/jit(cholesky)/cholesky | solution.py:67
  286.1 9.8 %custom-call.15 = f32[1,128,128]{1,2,0:T(8,128)S(1)} custom-call(f32[1,128,128]{2,1,0:T(8,128)S(1)} %get-tuple-element.53), custom_call_target="InvertDiagBlocksLowerTriangular" | custom-call | tf_op jit(solution)/shard_map/jit(cholesky)/cholesky | solution.py:67
  296.4 11.7 %cholesky.147 = f32[128,128]{1,0:T(8,128)S(1)} custom-call(f32[128,128]{1,0:T(8,128)S(1)} %convolution_subtract_fusion.1), custom_call_target="Cholesky" | custom-call | tf_op jit(solution)/shard_map/jit(cholesky)/cholesky | solution.py:67
  310.4 4.3 while.4
  314.6 19.7 %custom-call.16 = f32[2,128,128]{1,2,0:T(8,128)S(1)} custom-call(f32[2,128,128]{2,1,0:T(8,128)S(1)} %get-tuple-element.18), custom_call_target="InvertDiagBlocksLowerTriangular" | custom-call | tf_op jit(solution)/shard_map/jit(_solve_triangular)/triangular_solve | solution.py:68
  334.9 5.2 all_gather.18
  341.2 61.2 %reduce-scatter.5.cloned.1.call-done = f32[32,256]{1,0:T(8,128)} async-done(((f32[256,256]{1,0:T(8,128)}), f32[32,256]{1,0:T(8,128)}) %reduce-scatter.5.cloned.1.call-update) | async-done | bytes 32784 | tf_op jit(solution)/shard_map/reduce_scatter | solution.py:60
  405.1 128.9 %all-reduce.6.cloned.1.call-done = f32[256,256]{0,1:T(8,128)} async-done(((f32[256,256]{0,1:T(8,128)}), f32[256,256]{0,1:T(8,128)}) %all-reduce.6.cloned.1.call-update) | async-done | bytes 262160 | tf_op jit(solution)/shard_map/psum | solution.py:66
  536.1 11.7 %cholesky.164 = f32[128,128]{1,0:T(8,128)S(1)} custom-call(f32[128,128]{1,0:T(8,128)S(1)} %cholesky.197), custom_call_target="Cholesky" | custom-call | tf_op jit(solution)/shard_map/jit(cholesky)/cholesky | solution.py:67
  547.8 9.8 %custom-call.17 = f32[1,128,128]{1,2,0:T(8,128)S(1)} custom-call(f32[1,128,128]{2,1,0:T(8,128)S(1)} %get-tuple-element.49), custom_call_target="InvertDiagBlocksLowerTriangular" | custom-call | tf_op jit(solution)/shard_map/jit(cholesky)/cholesky | solution.py:67
  558.2 11.7 %cholesky.181 = f32[128,128]{1,0:T(8,128)S(1)} custom-call(f32[128,128]{1,0:T(8,128)S(1)} %convolution_subtract_fusion), custom_call_target="Cholesky" | custom-call | tf_op jit(solution)/shard_map/jit(cholesky)/cholesky | solution.py:67
  572.7 4.3 while.5
  577.0 19.7 %custom-call.18 = f32[2,128,128]{1,2,0:T(8,128)S(1)} custom-call(f32[2,128,128]{2,1,0:T(8,128)S(1)} %get-tuple-element.19), custom_call_target="InvertDiagBlocksLowerTriangular" | custom-call | tf_op jit(solution)/shard_map/jit(_solve_triangular)/triangular_solve | solution.py:68
  601.1 3.7 all-to-all-start
  607.4 6.2 fusion
  613.5 7.5 %all-to-all-done = bf16[32,32,256]{2,1,0:T(8,128)(2,1)S(1)} async-done(((bf16[32,32,256]{2,1,0:T(8,128)(2,1)}), bf16[32,32,256]{2,1,0:T(8,128)(2,1)S(1)}, u32[]{:S(2)}, u32[]{:S(2)}) %all-to-all-start) | async-done | bytes 524320 | tf_op jit(solution)/shard_map/all_to_all | solution.py:13
  621.0 4.4 divide_multiply_fusion
  (78 shorter events, 30.6 us)
Async XLA Ops:
  7.2 133.3 %reduce-scatter.3.cloned.1.call-start = ((), (), s32[]{:S(2)}) async-start(), calls=%async_computation.3 | async-start | bytes 294912 | tf_op jit(solution)/shard_map/reduce_scatter | solution.py:60
  80.7 191.5 %all-reduce.4.cloned.1.call-start = ((), (), s32[]{:S(2)}) async-start(), calls=%async_computation.4 | async-start | bytes 524288 | tf_op jit(solution)/shard_map/psum | solution.py:66
  140.4 193.9 %copy-start.2 = (f32[32,256]{1,0:T(8,128)S(1)}, f32[32,256]{1,0:T(8,128)}, u32[]{:S(2)}) copy-start(f32[32,256]{1,0:T(8,128)} %reduce-scatter.3.cloned.1.call-done) | copy-start | bytes 98308
  142.4 260.0 %reduce-scatter.5.cloned.1.call-start = ((), (), s32[]{:S(2)}) async-start(), calls=%async_computation.5 | async-start | bytes 294912 | tf_op jit(solution)/shard_map/reduce_scatter | solution.py:60
  341.1 263.7 %copy-start = (bf16[1024,1024]{1,0:T(8,128)(2,1)S(1)}, bf16[1024,1024]{1,0:T(8,128)(2,1)}, u32[]{:S(2)}) copy-start(bf16[1024,1024]{1,0:T(8,128)(2,1)} %param.8) | copy-start | bytes 6291460
  341.1 192.9 %all-reduce.6.cloned.1.call-start = ((), (), s32[]{:S(2)}) async-start(), calls=%async_computation.6 | async-start | bytes 524288 | tf_op jit(solution)/shard_map/psum | solution.py:66
  402.4 196.6 %copy-start.1 = (f32[32,256]{1,0:T(8,128)S(1)}, f32[32,256]{1,0:T(8,128)}, u32[]{:S(2)}) copy-start(f32[32,256]{1,0:T(8,128)} %reduce-scatter.5.cloned.1.call-done) | copy-start | bytes 98308
  404.4 200.9 %all-gather.2.cloned.1.call-start = ((), (), s32[]{:S(2)}) async-start(), calls=%async_computation.7 | async-start | bytes 2162688 | tf_op jit(solution)/shard_map/all_gather | solution.py:75
  601.1 19.9 %all-to-all-start = ((bf16[32,32,256]{2,1,0:T(8,128)(2,1)}), bf16[32,32,256]{2,1,0:T(8,128)(2,1)S(1)}, u32[]{:S(2)}, u32[]{:S(2)}) async-start(bf16[32,32,256]{2,1,0:T(8,128)(2,1)} %stack.2), calls=%async_computation.2 | async-start | bytes 1048576 | tf_op jit(solution)/shard_map/all_to_all | solution.py:13
Sparse Core Ops, SparseCore 0:
  80.9 59.5 reduce-scatter.2
  146.5 125.6 all-reduce.3
  341.2 61.1 reduce-scatter.4
  408.4 125.5 all-reduce.5
  536.8 56.2 all-gather.1
